TPU v7x, 32 devices: a whole 2x2x4 slice. The times are simulated.
32 devices in a mesh: dp: 2 (over core), expert: 4 (over y, x), mp: 4 (over z).
Axes of the slice: x: 2, y: 2, z: 4, core: 2. Of those that a mesh axis runs over, the one named last changes fastest.
Arguments:
- tokens: bfloat16 [512, 3072], P(('dp', 'expert')), may hold values from -6 to 6
- w_router: float32 [3072, 4], replicated, may hold values from -0.109375 to 0.109375
- expert_ids: int32 [512, 2], P(('dp', 'expert')), may hold values from 0 to 3, all different within a row; in each aligned block of 64 rows (0 to 63, 64 to 127, ...) at most 64 rows name the same one
- partner: int32 [4], replicated, may hold values from 0 to 3, as said below
- gate_weight: bfloat16 [4, 3072, 8192], P('expert', None, ('dp', 'mp')), may hold values from -0.109375 to 0.109375
- up_weight: bfloat16 [4, 3072, 8192], P('expert', None, ('dp', 'mp')), may hold values from -0.109375 to 0.109375
- down_weight: bfloat16 [4, 8192, 3072], P('expert', ('dp', 'mp')), may hold values from -0.0625 to 0.0625
- grad_out: bfloat16 [512, 3072], P(('dp', 'expert')), may hold values from -1.5 to 1.5
Outputs:
- mixed: bfloat16 [512, 3072], P(('dp', 'expert'))
- grad_tokens: bfloat16 [512, 3072], P(('dp', 'expert'))
- grad_router: float32 [3072, 4], replicated
- grad_gate: bfloat16 [4, 3072, 8192], P('expert', None, ('dp', 'mp'))
- grad_up: bfloat16 [4, 3072, 8192], P('expert', None, ('dp', 'mp'))
- grad_down: bfloat16 [4, 8192, 3072], P('expert', ('dp', 'mp'))
Inputs may be any that keep to these rules, and one draw needn't show every extreme that they name: `expert_ids`: each token names two different experts. Within each aligned block of 64 tokens no expert is named by more than 64 tokens, and in every draw some block names some expert exactly 64 times. A matching of the experts: partner[partner[e]] = e and partner[e] != e for every expert e.
All inputs are finite; a program needn't handle non-finite values.
Results may differ from a plain program's by a relative error of at most 0.019.
Values may be sent and summed in bfloat16 or wider, within the bound.
No kernel may reach another device: no remote copies, remote signals or barrier semaphores. Data moves between devices by JAX's collectives and lax.ppermute only.
A program may use at most 128 MiB of HBM per device.

v0:
```python
import jax
import jax.numpy as jnp
from jax import lax
from jax.sharding import PartitionSpec as P

exact_mode = lax.Precision.HIGHEST


def local(tokens, w_router, expert_ids, partner, gate_weight, up_weight, down_weight, grad_out):
    tok_rows, features = tokens.shape
    experts = w_router.shape[1]
    hid_part = gate_weight.shape[2]
    dp_count = lax.axis_size("dp")
    exp_count = lax.axis_size("expert")
    slot_count = min(tok_rows, 4 * tok_rows // experts)
    keep_count = 3 * slot_count // 4
    slot_total = experts * slot_count
    block_rows = exp_count * slot_count
    floats = tokens.astype(jnp.float32)
    logits = jnp.dot(floats, w_router, precision=exact_mode)
    chosen = (expert_ids[:, :, None] == lax.iota(jnp.int32, experts)[None, None, :]).astype(
        jnp.int32
    )
    chosen_float = chosen.astype(jnp.float32)
    picked = jnp.sum(logits[:, None, :] * chosen_float, axis=2)
    share_one = jax.nn.sigmoid(picked[:, 0] - picked[:, 1])
    shares = jnp.stack([share_one, 1.0 - share_one], axis=1)
    flat_choice = chosen.reshape(2 * tok_rows, experts)
    earlier = jnp.cumsum(flat_choice, axis=0) - flat_choice
    arrival = jnp.sum(earlier * flat_choice, axis=1).reshape(tok_rows, 2)
    partner_of = jnp.sum(chosen * partner[None, None, :], axis=2)
    target = jnp.where(arrival < keep_count, expert_ids, partner_of)
    slot_index = target * slot_count + arrival
    placing = (slot_index[:, :, None] == lax.iota(jnp.int32, slot_total)[None, None, :]).astype(
        jnp.bfloat16
    )
    send_tokens = jnp.einsum("tks,td->sd", placing, tokens, preferred_element_type=jnp.float32)
    send_tokens = send_tokens.astype(jnp.bfloat16).reshape(experts, slot_count, features)
    scaled = (shares[:, :, None] * grad_out.astype(jnp.float32)[:, None, :]).astype(jnp.bfloat16)
    send_cot = jnp.einsum("tks,tkd->sd", placing, scaled, preferred_element_type=jnp.float32)
    send_cot = send_cot.astype(jnp.bfloat16).reshape(experts, slot_count, features)

    def spread(buffer):
        arrived = lax.all_to_all(buffer, "expert", split_axis=0, concat_axis=0, tiled=True)
        return lax.all_gather(arrived, "dp", axis=0, tiled=True)

    rows_in = spread(send_tokens).reshape(-1, features)
    pieces = 1

    def combine(partial_value):
        summed = lax.psum(
            partial_value.reshape(dp_count, block_rows, features).astype(jnp.bfloat16), ("dp", "mp")
        ).astype(jnp.float32)
        own_rows = lax.dynamic_index_in_dim(summed, lax.axis_index("dp"), 0, keepdims=False)
        own_rows = own_rows.astype(jnp.bfloat16).reshape(exp_count, slot_count, features)
        restored = lax.all_to_all(own_rows, "expert", split_axis=0, concat_axis=0, tiled=True)
        return restored.reshape(slot_total, features)

    w_gate = gate_weight[0]
    w_up = up_weight[0]
    w_down = down_weight[0]
    pre_gate = jnp.dot(rows_in, w_gate, preferred_element_type=jnp.float32)
    pre_up = jnp.dot(rows_in, w_up, preferred_element_type=jnp.float32)
    sigmoid_gate = jax.nn.sigmoid(pre_gate)
    swished = pre_gate * sigmoid_gate
    hidden = (swished * pre_up).astype(jnp.bfloat16)
    down_split = w_down.reshape(hid_part, pieces, features // pieces)
    forward_terms = jnp.einsum(
        "prf,fqd->pqrd",
        hidden.reshape(dp_count, block_rows, hid_part),
        down_split,
        preferred_element_type=jnp.float32,
    )
    expert_out = combine(forward_terms)
    back_rows = jnp.einsum("tks,sd->tkd", placing, expert_out, preferred_element_type=jnp.float32)
    mixed = (shares[:, 0, None] * back_rows[:, 0] + shares[:, 1, None] * back_rows[:, 1]).astype(
        jnp.bfloat16
    )
    falling = grad_out.astype(jnp.float32)
    dshare = jnp.sum(falling[:, None, :] * back_rows, axis=2)
    dlogit = shares[:, 0] * shares[:, 1] * (dshare[:, 0] - dshare[:, 1])
    grad_logits = (chosen_float[:, 0] - chosen_float[:, 1]) * dlogit[:, None]
    router_term = lax.dot_general(
        floats, grad_logits, (((0,), (0,)), ((), ())), precision=exact_mode
    )
    grad_router = lax.psum(router_term.astype(jnp.bfloat16), ("dp", "expert")).astype(jnp.float32)
    router_back = jnp.dot(grad_logits, w_router.T, precision=exact_mode)
    cot_in = spread(send_cot).reshape(-1, features)
    dhidden = jnp.einsum("rd,fd->rf", cot_in, w_down, preferred_element_type=jnp.float32)
    up_grad = (dhidden * swished).astype(jnp.bfloat16)
    gate_grad = (dhidden * pre_up * sigmoid_gate * (1.0 + pre_gate * (1.0 - sigmoid_gate))).astype(
        jnp.bfloat16
    )
    grad_down = jnp.einsum("rf,rd->fd", hidden, cot_in, preferred_element_type=jnp.float32).astype(
        jnp.bfloat16
    )[None]
    grad_gate = jnp.einsum(
        "rd,rf->df", rows_in, gate_grad, preferred_element_type=jnp.float32
    ).astype(jnp.bfloat16)[None]
    grad_up = jnp.einsum("rd,rf->df", rows_in, up_grad, preferred_element_type=jnp.float32).astype(
        jnp.bfloat16
    )[None]
    gate_split = w_gate.reshape(pieces, features // pieces, hid_part)
    up_split = w_up.reshape(pieces, features // pieces, hid_part)
    backward_terms = jnp.einsum(
        "prf,qdf->pqrd",
        gate_grad.reshape(dp_count, block_rows, hid_part),
        gate_split,
        preferred_element_type=jnp.float32,
    )
    backward_terms = backward_terms + jnp.einsum(
        "prf,qdf->pqrd",
        up_grad.reshape(dp_count, block_rows, hid_part),
        up_split,
        preferred_element_type=jnp.float32,
    )
    row_grads = combine(backward_terms)
    grad_rows = jnp.einsum("tks,sd->tkd", placing, row_grads, preferred_element_type=jnp.float32)
    grad_tokens = (router_back + grad_rows[:, 0] + grad_rows[:, 1]).astype(jnp.bfloat16)
    return (mixed, grad_tokens, grad_router, grad_gate, grad_up, grad_down)


def solution(mesh):
    in_specs = (
        P(("dp", "expert"), None),
        P(),
        P(("dp", "expert"), None),
        P(),
        P("expert", None, ("dp", "mp")),
        P("expert", None, ("dp", "mp")),
        P("expert", ("dp", "mp"), None),
        P(("dp", "expert"), None),
    )
    out_specs = (
        P(("dp", "expert"), None),
        P(("dp", "expert"), None),
        P(),
        P("expert", None, ("dp", "mp")),
        P("expert", None, ("dp", "mp")),
        P("expert", ("dp", "mp"), None),
    )
    return jax.shard_map(local, mesh=mesh, in_specs=in_specs, out_specs=out_specs, check_vma=False)
```

profile of v0, /device:TPU:1, one launch (start us, length us, event | category | flops | bytes accessed | tf_op | source)
XLA Modules:
  0.0 329.8 jit_solution(508223752091180420)
XLA Ops:
  8.2 1.2 fusion.42
  14.2 22.7 %all_to_all.20 = bf16[4,64,3072]{2,1,0:T(8,128)(2,1)} all-to-all(bf16[4,64,3072]{2,1,0:T(8,128)(2,1)S(1)} %bitcast.108), channel_id=1, replica_groups=mesh['dp'=2,'expert'=4,'mp'=4] {'expert'}, dimensions={0} | all-to-all | bytes 3145728 | tf_op jit(solution)/shard_map/all_to_all | solution.py:44
  37.6 20.3 %all_to_all.21 = bf16[4,64,3072]{2,1,0:T(8,128)(2,1)} all-to-all(bf16[4,64,3072]{2,1,0:T(8,128)(2,1)S(1)} %bitcast.105), channel_id=1, replica_groups=mesh['dp'=2,'expert'=4,'mp'=4] {'expert'}, dimensions={0} | all-to-all | bytes 3145728 | tf_op jit(solution)/shard_map/all_to_all | solution.py:44
  58.0 6.5 %fusion.6 = f32[512,1024]{1,0:T(8,128)S(1)} fusion(bf16[512,3072]{1,0:T(8,128)(2,1)} %bitcast.120, bf16[1,1024,3072]{2,1,0:T(8,128)(2,1)} %param.14), kind=kOutput, calls=%fused_computation.6 | convolution fusion | flops 3221225472 | bytes 11534336 | tf_op jit(solution)/shard_map/rd,fd->rf/dot_general | solution.py:89
  64.6 8.7 %all-gather.3.cloned.1.call-done = bf16[8,64,3072]{2,1,0:T(8,128)(2,1)} async-done(((bf16[4,64,3072]{2,1,0:T(8,128)(2,1)}), bf16[8,64,3072]{2,1,0:T(8,128)(2,1)}) %all-gather.3.cloned.1.call-update) | async-done | bytes 3145744 | tf_op jit(solution)/shard_map/all_gather | solution.py:45
  73.3 6.6 %fusion.8 = f32[512,1024]{1,0:T(8,128)S(1)} fusion(bf16[512,3072]{1,0:T(8,128)(2,1)} %bitcast.116, bf16[1,3072,1024]{2,1,0:T(8,128)(2,1)} %param.13), kind=kOutput, calls=%fused_computation.8 | convolution fusion | flops 3221225472 | bytes 11534336 | tf_op jit(solution)/shard_map/dot_general | solution.py:63
  79.9 7.3 %multiply_convert_fusion.1 = (bf16[512,1024]{1,0:T(8,128)(2,1)S(1)}, bf16[512,1024]{1,0:T(8,128)(2,1)S(1)}, bf16[512,1024]{1,0:T(8,128)(2,1)S(1)}) fusion(f32[512,1024]{1,0:T(8,128)S(1)} %fusion.6, f32[512,1024]{1,0:T(8,128)S(1)} %fusion.8, bf16[512,3072]{1,0:T(8,128)(2,1)S(1)} %bitcast.118, bf16[1,3072,1024]{2,1,0:T(8,128)(2,1)} %param.12), kind=kOutput, calls=%fused_computation.28 | convolution fusion | flops 3229089792 | bytes 16777216 | tf_op jit(solution)/shard_map/dot_general | solution.py:62
  87.3 5.4 %fusion = f32[2,256,3072]{2,1,0:T(8,128)} fusion(bf16[2,256,1024]{2,1,0:T(8,128)(2,1)S(1)} %bitcast.123, bf16[1,3072,1024]{2,1,0:T(8,128)(2,1)S(1)} %bitcast.111), kind=kOutput, calls=%fused_computation | convolution fusion | flops 3221225472 | bytes 13631488 | tf_op jit(solution)/shard_map/prf,qdf->pqrd/dot_general | solution.py:111
  92.7 4.8 %fusion.14 = bf16[2,256,3072]{2,1,0:T(8,128)(2,1)} fusion(bf16[2,256,1024]{2,1,0:T(8,128)(2,1)S(1)} %bitcast.124, bf16[1,1024,3072]{2,1,0:T(8,128)(2,1)S(1)} %bitcast.113), kind=kOutput, calls=%fused_computation.16 | convolution fusion | flops 3222798336 | bytes 10485760 | tf_op jit(solution)/shard_map/prf,fqd->pqrd/dot_general | solution.py:68
  97.5 6.8 %add_convert_fusion = bf16[2,256,3072]{2,1,0:T(8,128)(2,1)} fusion(f32[2,256,3072]{2,1,0:T(8,128)} %fusion, bf16[2,256,1024]{2,1,0:T(8,128)(2,1)S(1)} %bitcast.122, bf16[1,3072,1024]{2,1,0:T(8,128)(2,1)S(1)} %bitcast.115), kind=kOutput, calls=%fused_computation.15 | convolution fusion | flops 3224371200 | bytes 16777216 | tf_op jit(solution)/shard_map/prf,qdf->pqrd/dot_general | solution.py:105
  104.4 137.3 %all-reduce.3.cloned.1.call-done = (bf16[2,256,3072]{2,1,0:T(8,128)(2,1)}, bf16[2,256,3072]{2,1,0:T(8,128)(2,1)}) async-done(((bf16[2,256,3072]{2,1,0:T(8,128)(2,1)}, bf16[2,256,3072]{2,1,0:T(8,128)(2,1)}), (bf16[2,256,3072]{2,1,0:T(8,128)(2,1)}, bf16[2,256,3072]{2,1,0:T(8,128)(2,1)})) %all-reduce.3.cloned.1.call-update) | async-done | bytes 6291472 | tf_op jit(solution)/shard_map/psum | solution.py:51
  241.6 2.7 convert_convert_fusion
  244.3 3.7 %all-to-all-start.3 = ((bf16[4,64,3072]{2,1,0:T(8,128)(2,1)}), bf16[4,64,3072]{2,1,0:T(8,128)(2,1)S(1)}, u32[]{:S(2)}, u32[]{:S(2)}) async-start(bf16[4,64,3072]{2,1,0:T(8,128)(2,1)} %bitcast.107), calls=%async_computation.3 | async-start | bytes 3145728 | tf_op jit(solution)/shard_map/all_to_all | solution.py:56
  248.1 8.5 %convert_bitcast_fusion = bf16[1,1024,3072]{2,1,0:T(8,128)(2,1)} fusion(bf16[512,1024]{1,0:T(8,128)(2,1)} %copy-done.10, bf16[512,3072]{1,0:T(8,128)(2,1)} %bitcast.121), kind=kOutput, calls=%fused_computation.12 | convolution fusion | flops 3224371200 | bytes 10485760 | tf_op jit(solution)/shard_map/rf,rd->fd/dot_general | solution.py:94
  256.6 1.3 convert_convert_fusion.1
  257.9 8.6 %all-to-all-done.3 = bf16[4,64,3072]{2,1,0:T(8,128)(2,1)S(1)} async-done(((bf16[4,64,3072]{2,1,0:T(8,128)(2,1)}), bf16[4,64,3072]{2,1,0:T(8,128)(2,1)S(1)}, u32[]{:S(2)}, u32[]{:S(2)}) %all-to-all-start.3) | async-done | bytes 1572896 | tf_op jit(solution)/shard_map/all_to_all | solution.py:56
  266.6 4.4 %all-to-all-start.1 = ((bf16[4,64,3072]{2,1,0:T(8,128)(2,1)}), bf16[4,64,3072]{2,1,0:T(8,128)(2,1)}, u32[]{:S(2)}, u32[]{:S(2)}) async-start(bf16[4,64,3072]{2,1,0:T(8,128)(2,1)} %bitcast.106), calls=%async_computation.1 | async-start | bytes 3145728 | tf_op jit(solution)/shard_map/all_to_all | solution.py:56
  270.9 8.5 %convert_bitcast_fusion.1 = bf16[1,3072,1024]{2,1,0:T(8,128)(2,1)} fusion(bf16[512,3072]{1,0:T(8,128)(2,1)} %bitcast.117, bf16[512,1024]{1,0:T(8,128)(2,1)} %copy-done.9), kind=kOutput, calls=%fused_computation.13 | convolution fusion | flops 3224371200 | bytes 10485760 | tf_op jit(solution)/shard_map/rd,rf->df/dot_general | solution.py:100
  279.5 5.4 %convert_bitcast_fusion.2 = bf16[1,3072,1024]{2,1,0:T(8,128)(2,1)} fusion(bf16[512,3072]{1,0:T(8,128)(2,1)S(1)} %bitcast.119, bf16[512,1024]{1,0:T(8,128)(2,1)S(1)} %copy-done.8), kind=kOutput, calls=%fused_computation.14 | convolution fusion | flops 3224371200 | bytes 10485760 | tf_op jit(solution)/shard_map/rd,rf->df/dot_general | solution.py:97
  284.8 1.6 fusion.28
  286.4 3.3 all-to-all-done.1
  289.7 2.1 multiply_reduce_fusion
  292.0 1.6 fusion.19
  293.7 28.0 %psum.23 = bf16[3072,4]{0,1:T(4,128)(2,1)S(1)} all-reduce(bf16[3072,4]{0,1:T(4,128)(2,1)S(1)} %fusion.20), channel_id=1, replica_groups=mesh['dp'=2,'expert'=4,'mp'=4] {'dp','expert'}, use_global_device_ids=true, to_apply=%region_8.9 | all-reduce | flops 12288 | bytes 49152 | tf_op jit(solution)/shard_map/psum | solution.py:86
  (66 shorter events, 8.5 us)
Async XLA Ops:
  7.2 1.0 copy-start
  7.2 50.8 %all-gather.5.cloned.1.call-start = ((), (), s32[]{:S(2)}) async-start(), calls=%async_computation.5 | async-start | bytes 4718592 | tf_op jit(solution)/shard_map/all_gather | solution.py:45
  36.9 36.4 %all-gather.3.cloned.1.call-start = ((), (), s32[]{:S(2)}) async-start(), calls=%async_computation.4 | async-start | bytes 4718592 | tf_op jit(solution)/shard_map/all_gather | solution.py:45
  57.9 183.7 %all-reduce.3.cloned.1.call-start = ((), (), s32[]{:S(2)}) async-start(), calls=%async_computation.6 | async-start | bytes 12582912 | tf_op jit(solution)/shard_map/psum | solution.py:51
  73.3 6.6 %copy-start.5 = (bf16[8,64,3072]{2,1,0:T(8,128)(2,1)S(1)}, bf16[8,64,3072]{2,1,0:T(8,128)(2,1)}, u32[]{:S(2)}) copy-start(bf16[8,64,3072]{2,1,0:T(8,128)(2,1)} %all-gather.3.cloned.1.call-done) | copy-start | bytes 9437188
  73.3 14.0 %slice-start = ((s8[6291456]{0:T(1024)(128)(4,1)}), s8[4194304]{0:T(1024)(128)(4,1)S(1)}, s32[]{:S(2)}) async-start(s8[6291456]{0:T(1024)(128)(4,1)} %bitcast.110), calls=%async_computation.7 | async-start | bytes 8388608
  73.3 19.4 %slice-start.2 = ((s8[6291456]{0:T(1024)(128)(4,1)}), s8[4194304]{0:T(1024)(128)(4,1)S(1)}, s32[]{:S(2)}) async-start(s8[6291456]{0:T(1024)(128)(4,1)} %bitcast.112), calls=%async_computation.9 | async-start | bytes 8388608
  79.9 7.4 %slice-start.1 = ((s8[6291456]{0:T(1024)(128)(4,1)}), s8[2097152]{0:T(1024)(128)(4,1)S(1)}, s32[]{:S(2)}) async-start(s8[6291456]{0:T(1024)(128)(4,1)} %bitcast.110), calls=%async_computation.8 | async-start | bytes 4194304
  79.9 12.8 %slice-start.3 = ((s8[6291456]{0:T(1024)(128)(4,1)}), s8[2097152]{0:T(1024)(128)(4,1)S(1)}, s32[]{:S(2)}) async-start(s8[6291456]{0:T(1024)(128)(4,1)} %bitcast.112), calls=%async_computation.10 | async-start | bytes 4194304
  79.9 17.6 %slice-start.4 = ((s8[6291456]{0:T(1024)(128)(4,1)}), s8[4194304]{0:T(1024)(128)(4,1)S(1)}, s32[]{:S(2)}) async-start(s8[6291456]{0:T(1024)(128)(4,1)} %bitcast.114), calls=%async_computation.11 | async-start | bytes 8388608
  87.2 5.4 %copy-start.9 = (bf16[512,1024]{1,0:T(8,128)(2,1)}, bf16[512,1024]{1,0:T(8,128)(2,1)S(1)}, u32[]{:S(2)}) copy-start(bf16[512,1024]{1,0:T(8,128)(2,1)S(1)} %get-tuple-element.11) | copy-start | bytes 3145732
  87.2 5.4 %copy-start.10 = (bf16[512,1024]{1,0:T(8,128)(2,1)}, bf16[512,1024]{1,0:T(8,128)(2,1)S(1)}, u32[]{:S(2)}) copy-start(bf16[512,1024]{1,0:T(8,128)(2,1)S(1)} %get-tuple-element.12) | copy-start | bytes 3145732
  87.2 10.3 %copy-start.7 = (bf16[512,1024]{1,0:T(8,128)(2,1)}, bf16[512,1024]{1,0:T(8,128)(2,1)S(1)}, u32[]{:S(2)}) copy-start(bf16[512,1024]{1,0:T(8,128)(2,1)S(1)} %get-tuple-element.10) | copy-start | bytes 3145732
  87.3 10.2 %slice-start.5 = ((s8[6291456]{0:T(1024)(128)(4,1)}), s8[2097152]{0:T(1024)(128)(4,1)S(1)}, s32[]{:S(2)}) async-start(s8[6291456]{0:T(1024)(128)(4,1)} %bitcast.114), calls=%async_computation.12 | async-start | bytes 4194304
  241.6 6.4 %copy-start.4 = (s32[64,2]{0,1:T(2,128)S(1)}, s32[64,2]{0,1:T(2,128)}, u32[]{:S(2)}) copy-start(s32[64,2]{0,1:T(2,128)} %param.10) | copy-start | bytes 1540
  244.3 22.3 %all-to-all-start.3 = ((bf16[4,64,3072]{2,1,0:T(8,128)(2,1)}), bf16[4,64,3072]{2,1,0:T(8,128)(2,1)S(1)}, u32[]{:S(2)}, u32[]{:S(2)}) async-start(bf16[4,64,3072]{2,1,0:T(8,128)(2,1)} %bitcast.107), calls=%async_computation.3 | async-start | bytes 3145728 | tf_op jit(solution)/shard_map/all_to_all | solution.py:56
  248.1 8.6 %copy-start.2 = (bf16[2,256,3072]{2,1,0:T(8,128)(2,1)S(1)}, bf16[2,256,3072]{2,1,0:T(8,128)(2,1)}, u32[]{:S(2)}) copy-start(bf16[2,256,3072]{2,1,0:T(8,128)(2,1)} %get-tuple-element.6) | copy-start | bytes 9437188
  266.6 23.1 %all-to-all-start.1 = ((bf16[4,64,3072]{2,1,0:T(8,128)(2,1)}), bf16[4,64,3072]{2,1,0:T(8,128)(2,1)}, u32[]{:S(2)}, u32[]{:S(2)}) async-start(bf16[4,64,3072]{2,1,0:T(8,128)(2,1)} %bitcast.106), calls=%async_computation.1 | async-start | bytes 3145728 | tf_op jit(solution)/shard_map/all_to_all | solution.py:56
  270.9 8.5 %copy-start.6 = (bf16[8,64,3072]{2,1,0:T(8,128)(2,1)S(1)}, bf16[8,64,3072]{2,1,0:T(8,128)(2,1)}, u32[]{:S(2)}) copy-start(bf16[8,64,3072]{2,1,0:T(8,128)(2,1)} %all-gather.3.cloned.1.call-done) | copy-start | bytes 9437188
  270.9 8.5 %copy-start.8 = (bf16[512,1024]{1,0:T(8,128)(2,1)S(1)}, bf16[512,1024]{1,0:T(8,128)(2,1)}, u32[]{:S(2)}) copy-start(bf16[512,1024]{1,0:T(8,128)(2,1)} %copy-done.7) | copy-start | bytes 3145732
  284.8 7.2 %copy-start.3 = (f32[3072,4]{0,1:T(4,128)S(1)}, f32[3072,4]{0,1:T(4,128)}, u32[]{:S(2)}) copy-start(f32[3072,4]{0,1:T(4,128)} %param.9) | copy-start | bytes 147460
  289.7 2.4 copy-start.1
Sparse Core Ops, SparseCore 0:
  37.0 13.7 all-gather.4
  58.1 15.1 all-gather.2
  104.5 137.1 all-reduce.2
where the time goes:
time: 330 us
  waiting for transfers between devices  158 us (48%)
  blocking collectives  71 us (22%)
  matrix products  67.8 us (21%)
  between operations  14.1 us (4%)
  other arithmetic  9.3 us (3%)
  starting transfers between devices  8.22 us (2%)
    psum x1, waiting for transfers between devices, combine(): lax.psum(partial_value.reshape(dp_count, block_rows, features).astype(jnp...  137 us
    all_to_all x2, blocking collectives, spread(): lax.all_to_all(buffer, 'expert', split_axis=0, concat_axis=0, tiled=True)  43 us
    psum x1, blocking collectives, local(): lax.psum(router_term.astype(jnp.bfloat16), ('dp', 'expert'))  28 us
    all_to_all x2, waiting for transfers between devices, combine(): lax.all_to_all(own_rows, 'expert', split_axis=0, concat_axis=0, tiled=True)  11.9 us
    all_gather x2, waiting for transfers between devices, spread(): return lax.all_gather(arrived, 'dp', axis=0, tiled=True)  8.71 us
    dot_general x1, matrix products, local(): jnp.einsum('rf,rd->fd', hidden, cot_in, preferred_element_type=jnp.float32)  8.54 us
    dot_general x1, matrix products, local(): jnp.einsum('rd,rf->df', rows_in, up_grad, preferred_element_type=jnp.floa...  8.5 us
    all_to_all x2, starting transfers between devices, combine(): lax.all_to_all(own_rows, 'expert', split_axis=0, concat_axis=0, tiled=True)  8.1 us
  transfers between devices with their start and end apart: 5, of which 4 were waited for; matrix products, arithmetic and copies ran while one was open for 10% of the time, Pallas kernels for 0%

commit v1 on v0

--- a/solution.py
+++ b/solution.py
@@ -49,7 +49,10 @@
 
     def combine(partial_value):
         summed = lax.psum(
-            partial_value.reshape(dp_count, block_rows, features).astype(jnp.bfloat16), ("dp", "mp")
+            lax.psum(
+                partial_value.reshape(dp_count, block_rows, features).astype(jnp.bfloat16), "mp"
+            ),
+            "dp",
         ).astype(jnp.float32)
         own_rows = lax.dynamic_index_in_dim(summed, lax.axis_index("dp"), 0, keepdims=False)
         own_rows = own_rows.astype(jnp.bfloat16).reshape(exp_count, slot_count, features)

time: 330 us -> 445 us (1.35)
  waiting for transfers between devices: 158 us -> 277 us
    psum x1, waiting for transfers between devices: 137 us -> 224 us  [combine(): lax.psum(partial_value.reshape(dp_count, block_rows, features).astype(jnp...]
    psum x0 -> x1, waiting for transfers between devices: none -> 33.8 us  [combine(): lax.psum(lax.psum(partial_value.reshape(dp_count, block_rows, features).a...]
  transfers between devices with their start and end apart: 5 -> 6, of which waited for: 4 -> 5; matrix products, arithmetic and copies ran while one was open for 10% -> 8% of each run, Pallas kernels for 0% -> 0%
where the time goes in v1:
time: 445 us
  waiting for transfers between devices  277 us (62%)
  blocking collectives  71 us (16%)
  matrix products  63.4 us (14%)
  between operations  14.1 us (3%)
  other arithmetic  9.31 us (2%)
  starting transfers between devices  8.32 us (2%)
    psum x1, waiting for transfers between devices, combine(): lax.psum(partial_value.reshape(dp_count, block_rows, features).astype(jnp...  224 us
    all_to_all x2, blocking collectives, spread(): lax.all_to_all(buffer, 'expert', split_axis=0, concat_axis=0, tiled=True)  43 us
    psum x1, waiting for transfers between devices, combine(): lax.psum(lax.psum(partial_value.reshape(dp_count, block_rows, features).a...  33.8 us
    psum x1, blocking collectives, local(): lax.psum(router_term.astype(jnp.bfloat16), ('dp', 'expert'))  28 us
    all_to_all x2, waiting for transfers between devices, combine(): lax.all_to_all(own_rows, 'expert', split_axis=0, concat_axis=0, tiled=True)  12.4 us
  transfers between devices with their start and end apart: 6, of which 5 were waited for; matrix products, arithmetic and copies ran while one was open for 8% of the time, Pallas kernels for 0%

profile of v1, /device:TPU:1, one launch (start us, length us, event | category | flops | bytes accessed | tf_op | source)
XLA Modules:
  0.0 444.5 jit_solution(12461712634632548116)
XLA Ops:
  14.2 22.7 %all_to_all.20 = bf16[4,64,3072]{2,1,0:T(8,128)(2,1)} all-to-all(bf16[4,64,3072]{2,1,0:T(8,128)(2,1)S(1)} %bitcast.108), channel_id=1, replica_groups=mesh['dp'=2,'expert'=4,'mp'=4] {'expert'}, dimensions={0} | all-to-all | bytes 3145728 | tf_op jit(solution)/shard_map/all_to_all | solution.py:44
  37.6 20.3 %all_to_all.21 = bf16[4,64,3072]{2,1,0:T(8,128)(2,1)} all-to-all(bf16[4,64,3072]{2,1,0:T(8,128)(2,1)S(1)} %bitcast.105), channel_id=1, replica_groups=mesh['dp'=2,'expert'=4,'mp'=4] {'expert'}, dimensions={0} | all-to-all | bytes 3145728 | tf_op jit(solution)/shard_map/all_to_all | solution.py:44
  58.0 8.6 %fusion.6 = f32[512,1024]{1,0:T(8,128)} fusion(bf16[512,3072]{1,0:T(8,128)(2,1)} %bitcast.120, bf16[1,1024,3072]{2,1,0:T(8,128)(2,1)} %param.14), kind=kOutput, calls=%fused_computation.6 | convolution fusion | flops 3221225472 | bytes 11534336 | tf_op jit(solution)/shard_map/rd,fd->rf/dot_general | solution.py:92
  66.7 6.6 %all-gather.3.cloned.1.call-done = bf16[8,64,3072]{2,1,0:T(8,128)(2,1)} async-done(((bf16[4,64,3072]{2,1,0:T(8,128)(2,1)}), bf16[8,64,3072]{2,1,0:T(8,128)(2,1)}) %all-gather.3.cloned.1.call-update) | async-done | bytes 3145744 | tf_op jit(solution)/shard_map/all_gather | solution.py:45
  73.3 6.8 %fusion.8 = f32[512,1024]{1,0:T(8,128)S(1)} fusion(bf16[512,3072]{1,0:T(8,128)(2,1)} %bitcast.116, bf16[1,3072,1024]{2,1,0:T(8,128)(2,1)} %param.13), kind=kOutput, calls=%fused_computation.8 | convolution fusion | flops 3221225472 | bytes 11534336 | tf_op jit(solution)/shard_map/dot_general | solution.py:66
  80.1 4.4 multiply_convert_fusion.1
  84.6 3.5 fusion
  88.1 4.8 %fusion.14 = bf16[2,256,3072]{2,1,0:T(8,128)(2,1)} fusion(bf16[2,256,1024]{2,1,0:T(8,128)(2,1)S(1)} %bitcast.124, bf16[1,1024,3072]{2,1,0:T(8,128)(2,1)S(1)} %bitcast.113), kind=kOutput, calls=%fused_computation.16 | convolution fusion | flops 3222798336 | bytes 10485760 | tf_op jit(solution)/shard_map/prf,fqd->pqrd/dot_general | solution.py:71
  92.9 5.0 %add_convert_fusion = bf16[2,256,3072]{2,1,0:T(8,128)(2,1)} fusion(f32[2,256,3072]{2,1,0:T(8,128)S(1)} %fusion, bf16[2,256,1024]{2,1,0:T(8,128)(2,1)S(1)} %bitcast.122, bf16[1,3072,1024]{2,1,0:T(8,128)(2,1)S(1)} %bitcast.115), kind=kOutput, calls=%fused_computation.15 | convolution fusion | flops 3224371200 | bytes 16777216 | tf_op jit(solution)/shard_map/prf,qdf->pqrd/dot_general | solution.py:108
  97.9 224.1 %all-reduce.5.cloned.1.call-done = (bf16[2,256,3072]{2,1,0:T(8,128)(2,1)}, bf16[2,256,3072]{2,1,0:T(8,128)(2,1)}) async-done(((bf16[2,256,3072]{2,1,0:T(8,128)(2,1)}, bf16[2,256,3072]{2,1,0:T(8,128)(2,1)}), (bf16[2,256,3072]{2,1,0:T(8,128)(2,1)}, bf16[2,256,3072]{2,1,0:T(8,128)(2,1)})) %all-reduce.5.cloned.1.call-update) | async-done | bytes 6291472 | tf_op jit(solution)/shard_map/psum | solution.py:52
  322.1 33.8 %all-reduce.7.cloned.1.call-done = (bf16[2,256,3072]{2,1,0:T(8,128)(2,1)}, bf16[2,256,3072]{2,1,0:T(8,128)(2,1)}) async-done(((bf16[2,256,3072]{2,1,0:T(8,128)(2,1)}, bf16[2,256,3072]{2,1,0:T(8,128)(2,1)}), (bf16[2,256,3072]{2,1,0:T(8,128)(2,1)}, bf16[2,256,3072]{2,1,0:T(8,128)(2,1)})) %all-reduce.7.cloned.1.call-update) | async-done | bytes 6291472 | tf_op jit(solution)/shard_map/psum | solution.py:51
  355.8 2.7 convert_convert_fusion
  358.5 3.8 all-to-all-start.3
  362.3 8.5 %convert_bitcast_fusion = bf16[1,1024,3072]{2,1,0:T(8,128)(2,1)} fusion(bf16[512,1024]{1,0:T(8,128)(2,1)} %copy-done.10, bf16[512,3072]{1,0:T(8,128)(2,1)} %bitcast.121), kind=kOutput, calls=%fused_computation.12 | convolution fusion | flops 3224371200 | bytes 10485760 | tf_op jit(solution)/shard_map/rf,rd->fd/dot_general | solution.py:97
  370.9 1.3 convert_convert_fusion.1
  372.2 9.2 %all-to-all-done.3 = bf16[4,64,3072]{2,1,0:T(8,128)(2,1)S(1)} async-done(((bf16[4,64,3072]{2,1,0:T(8,128)(2,1)}), bf16[4,64,3072]{2,1,0:T(8,128)(2,1)S(1)}, u32[]{:S(2)}, u32[]{:S(2)}) %all-to-all-start.3) | async-done | bytes 1572896 | tf_op jit(solution)/shard_map/all_to_all | solution.py:59
  381.3 4.4 all-to-all-start.1
  385.7 8.5 %convert_bitcast_fusion.1 = bf16[1,3072,1024]{2,1,0:T(8,128)(2,1)} fusion(bf16[512,3072]{1,0:T(8,128)(2,1)} %bitcast.117, bf16[512,1024]{1,0:T(8,128)(2,1)} %copy-done.9), kind=kOutput, calls=%fused_computation.13 | convolution fusion | flops 3224371200 | bytes 10485760 | tf_op jit(solution)/shard_map/rd,rf->df/dot_general | solution.py:103
  394.3 5.4 %convert_bitcast_fusion.2 = bf16[1,3072,1024]{2,1,0:T(8,128)(2,1)} fusion(bf16[512,3072]{1,0:T(8,128)(2,1)S(1)} %bitcast.119, bf16[512,1024]{1,0:T(8,128)(2,1)S(1)} %copy-done.8), kind=kOutput, calls=%fused_computation.14 | convolution fusion | flops 3224371200 | bytes 10485760 | tf_op jit(solution)/shard_map/rd,rf->df/dot_general | solution.py:100
  399.6 1.6 fusion.28
  401.2 3.3 all-to-all-done.1
  404.5 2.0 multiply_reduce_fusion
  406.8 1.6 fusion.19
  408.5 28.0 %psum.39 = bf16[3072,4]{0,1:T(4,128)(2,1)S(1)} all-reduce(bf16[3072,4]{0,1:T(4,128)(2,1)S(1)} %fusion.20), channel_id=1, replica_groups=mesh['dp'=2,'expert'=4,'mp'=4] {'dp','expert'}, use_global_device_ids=true, to_apply=%region_10.11 | all-reduce | flops 12288 | bytes 49152 | tf_op jit(solution)/shard_map/psum | solution.py:89
  (71 shorter events, 9.7 us)
Async XLA Ops:
  7.2 1.0 copy-start
  7.2 50.8 %all-gather.5.cloned.1.call-start = ((), (), s32[]{:S(2)}) async-start(), calls=%async_computation.5 | async-start | bytes 4718592 | tf_op jit(solution)/shard_map/all_gather | solution.py:45
  36.9 36.4 %all-gather.3.cloned.1.call-start = ((), (), s32[]{:S(2)}) async-start(), calls=%async_computation.4 | async-start | bytes 4718592 | tf_op jit(solution)/shard_map/all_gather | solution.py:45
  57.9 264.1 %all-reduce.5.cloned.1.call-start = ((), (), s32[]{:S(2)}) async-start(), calls=%async_computation.6 | async-start | bytes 12582912 | tf_op jit(solution)/shard_map/psum | solution.py:52
  58.0 22.0 %slice-start.4 = ((s8[6291456]{0:T(1024)(128)(4,1)}), s8[2097152]{0:T(1024)(128)(4,1)S(1)}, s32[]{:S(2)}) async-start(s8[6291456]{0:T(1024)(128)(4,1)} %bitcast.114), calls=%async_computation.12 | async-start | bytes 4194304
  73.3 6.8 %slice-start.5 = ((s8[6291456]{0:T(1024)(128)(4,1)}), s8[4194304]{0:T(1024)(128)(4,1)S(1)}, s32[]{:S(2)}) async-start(s8[6291456]{0:T(1024)(128)(4,1)} %bitcast.114), calls=%async_computation.13 | async-start | bytes 8388608
  73.3 6.8 %copy-start.5 = (bf16[8,64,3072]{2,1,0:T(8,128)(2,1)S(1)}, bf16[8,64,3072]{2,1,0:T(8,128)(2,1)}, u32[]{:S(2)}) copy-start(bf16[8,64,3072]{2,1,0:T(8,128)(2,1)} %all-gather.3.cloned.1.call-done) | copy-start | bytes 9437188
  73.3 6.8 %copy-start.11 = (f32[512,1024]{1,0:T(8,128)S(1)}, f32[512,1024]{1,0:T(8,128)}, u32[]{:S(2)}) copy-start(f32[512,1024]{1,0:T(8,128)} %fusion.6) | copy-start | bytes 6291460
  73.3 11.3 %slice-start = ((s8[6291456]{0:T(1024)(128)(4,1)}), s8[4194304]{0:T(1024)(128)(4,1)S(1)}, s32[]{:S(2)}) async-start(s8[6291456]{0:T(1024)(128)(4,1)} %bitcast.110), calls=%async_computation.8 | async-start | bytes 8388608
  73.3 14.8 %slice-start.2 = ((s8[6291456]{0:T(1024)(128)(4,1)}), s8[4194304]{0:T(1024)(128)(4,1)S(1)}, s32[]{:S(2)}) async-start(s8[6291456]{0:T(1024)(128)(4,1)} %bitcast.112), calls=%async_computation.10 | async-start | bytes 8388608
  80.1 4.4 slice-start.1
  80.1 7.9 %slice-start.3 = ((s8[6291456]{0:T(1024)(128)(4,1)}), s8[2097152]{0:T(1024)(128)(4,1)S(1)}, s32[]{:S(2)}) async-start(s8[6291456]{0:T(1024)(128)(4,1)} %bitcast.112), calls=%async_computation.11 | async-start | bytes 4194304
  84.5 3.5 copy-start.9
  84.5 3.5 copy-start.10
  84.5 8.3 %copy-start.7 = (bf16[512,1024]{1,0:T(8,128)(2,1)}, bf16[512,1024]{1,0:T(8,128)(2,1)S(1)}, u32[]{:S(2)}) copy-start(bf16[512,1024]{1,0:T(8,128)(2,1)S(1)} %get-tuple-element.12) | copy-start | bytes 3145732
  97.9 258.0 %all-reduce.7.cloned.1.call-start = ((), (), s32[]{:S(2)}) async-start(), calls=%async_computation.7 | async-start | bytes 12582912 | tf_op jit(solution)/shard_map/psum | solution.py:51
  355.8 6.5 %copy-start.4 = (s32[64,2]{0,1:T(2,128)S(1)}, s32[64,2]{0,1:T(2,128)}, u32[]{:S(2)}) copy-start(s32[64,2]{0,1:T(2,128)} %param.10) | copy-start | bytes 1540
  358.5 22.8 %all-to-all-start.3 = ((bf16[4,64,3072]{2,1,0:T(8,128)(2,1)}), bf16[4,64,3072]{2,1,0:T(8,128)(2,1)S(1)}, u32[]{:S(2)}, u32[]{:S(2)}) async-start(bf16[4,64,3072]{2,1,0:T(8,128)(2,1)} %bitcast.107), calls=%async_computation.3 | async-start | bytes 3145728 | tf_op jit(solution)/shard_map/all_to_all | solution.py:59
  362.3 8.6 %copy-start.2 = (bf16[2,256,3072]{2,1,0:T(8,128)(2,1)S(1)}, bf16[2,256,3072]{2,1,0:T(8,128)(2,1)}, u32[]{:S(2)}) copy-start(bf16[2,256,3072]{2,1,0:T(8,128)(2,1)} %get-tuple-element.8) | copy-start | bytes 9437188
  381.3 23.1 %all-to-all-start.1 = ((bf16[4,64,3072]{2,1,0:T(8,128)(2,1)}), bf16[4,64,3072]{2,1,0:T(8,128)(2,1)}, u32[]{:S(2)}, u32[]{:S(2)}) async-start(bf16[4,64,3072]{2,1,0:T(8,128)(2,1)} %bitcast.106), calls=%async_computation.1 | async-start | bytes 3145728 | tf_op jit(solution)/shard_map/all_to_all | solution.py:59
  385.7 8.5 %copy-start.6 = (bf16[8,64,3072]{2,1,0:T(8,128)(2,1)S(1)}, bf16[8,64,3072]{2,1,0:T(8,128)(2,1)}, u32[]{:S(2)}) copy-start(bf16[8,64,3072]{2,1,0:T(8,128)(2,1)} %all-gather.3.cloned.1.call-done) | copy-start | bytes 9437188
  385.7 8.5 %copy-start.8 = (bf16[512,1024]{1,0:T(8,128)(2,1)S(1)}, bf16[512,1024]{1,0:T(8,128)(2,1)}, u32[]{:S(2)}) copy-start(bf16[512,1024]{1,0:T(8,128)(2,1)} %copy-done.7) | copy-start | bytes 3145732
  399.6 7.2 %copy-start.3 = (f32[3072,4]{0,1:T(4,128)S(1)}, f32[3072,4]{0,1:T(4,128)}, u32[]{:S(2)}) copy-start(f32[3072,4]{0,1:T(4,128)} %param.9) | copy-start | bytes 147460
  404.5 2.3 copy-start.1
Sparse Core Ops, SparseCore 0:
  37.0 13.7 all-gather.4
  58.1 15.1 all-gather.2
  98.0 224.0 all-reduce.4
  324.4 31.3 all-reduce.6
